TPU v7x, 32 devices: a whole 2x2x4 slice. The times are simulated.
32 devices in a mesh: gx: 4 (over y, core), gy: 8 (over z, x).
Axes of the slice: x: 2, y: 2, z: 4, core: 2. Of those that a mesh axis runs over, the one named last changes fastest.
Arguments:
- local_schur: float32 [4096, 8192], P('gx', 'gy'), as said below
- boundary_map: int32 [4, 8, 1024], P('gx', 'gy'), may hold values from 0 to 1023, each once within a row
- order_first: int32 [2, 8, 256], P(None, 'gy'), may hold values from 0 to 255, each once within a row
- order_second: int32 [2, 4, 512], replicated, may hold values from 0 to 511, each once within a row
Outputs:
- first_factor: float32 [512, 2048], P('gx', 'gy')
- first_panel: float32 [3072, 2048], P('gx', 'gy')
- second_factor: float32 [1024, 2048], P('gx', 'gy')
- second_panel: float32 [2048, 4096], P('gx', 'gy')
- merged_schur: float32 [2048, 16384], P('gx', 'gy')
Inputs may be any that keep to these rules, and one draw needn't show every extreme that they name: `local_schur`: each 1024 x 1024 block is symmetric positive definite. `boundary_map`: the 1024 slots of a subdomain hold each of its boundary nodes once. `order_first`: each row lists the 256 nodes of one separator once each. `order_second`: each row lists the 512 nodes of one separator once each.
All inputs are finite; a program needn't handle non-finite values.
Results may differ from a plain program's by a relative error of at most 0.0001.
Values sent between devices are 32-bit elements; how exact they have to be, the bound alone decides.
A program may use at most 128 MiB of HBM per device.

v0:
```python
import jax
import jax.numpy as jnp
from jax import lax
from jax.sharding import PartitionSpec as P

SEP = 256


highest = lax.Precision.HIGHEST


def partner(block, axis, stride):
    count = lax.axis_size(axis)
    route = []
    for low in range(count):
        high = low | 1 << stride
        if high != low and high < count:
            route += [(low, high), (high, low)]
    return lax.ppermute(block, axis, route)


def reorder(sub_block, slots, left_side, upper_side):
    edge_index = slots // SEP
    west_pos = jnp.where(left_side, 1, 0).astype(jnp.int32)
    north_pos = jnp.where(upper_side, 2, 3).astype(jnp.int32)
    new_edge = jnp.where(
        edge_index == 0,
        west_pos,
        jnp.where(
            edge_index == 1, 1 - west_pos, jnp.where(edge_index == 2, north_pos, 5 - north_pos)
        ),
    )
    target = new_edge * SEP + slots % SEP
    inverse = jnp.zeros_like(target).at[target].set(jnp.arange(target.shape[0], dtype=jnp.int32))
    return sub_block[inverse][:, inverse]


def gram_rows(left_rows, right_rows):
    return jnp.einsum(
        "ik,jk->ij", left_rows, right_rows, precision=highest, preferred_element_type=jnp.float32
    )


def panel_solve(factor, coupling):
    return lax.linalg.triangular_solve(
        factor, coupling, left_side=False, lower=True, transpose_a=True
    )


def stack_pair(own_part, other_part, own_first):
    return jnp.where(
        own_first,
        jnp.concatenate([own_part, other_part], axis=0),
        jnp.concatenate([other_part, own_part], axis=0),
    )


def place_side(own_part, own_first):
    zero_part = jnp.zeros_like(own_part)
    return jnp.where(
        own_first,
        jnp.concatenate([own_part, zero_part], axis=1),
        jnp.concatenate([zero_part, own_part], axis=1),
    )


def body(local_schur, boundary_map, order_first, order_second):
    row_count = lax.axis_size("gx")
    col_count = lax.axis_size("gy")
    row_bit = row_count.bit_length() - 2
    col_bit = col_count.bit_length() - 2
    pair_rows = row_count // 2
    pair_cols = col_count // 2
    row_index = lax.axis_index("gx")
    col_index = lax.axis_index("gy")
    upper_half = row_index < pair_rows
    left_half = col_index < pair_cols
    row_high = jnp.where(upper_half, 0, 1).astype(jnp.int32)
    col_high = jnp.where(left_half, 0, 1).astype(jnp.int32)
    pair_row = row_index % pair_rows
    pair_col = col_index % pair_cols
    inner_rows = 3 * SEP
    ordered = reorder(local_schur, boundary_map[0, 0], left_half, upper_half)
    own_block = ordered[:inner_rows, :inner_rows]
    coupling = ordered[:inner_rows, inner_rows:]
    shared = ordered[inner_rows:, inner_rows:]
    shared_other, coupling_other = partner((shared, coupling), "gx", row_bit)
    order_one = order_first[pair_row, 0]
    pivot_one = shared + shared_other
    factor_one = jnp.linalg.cholesky(pivot_one[order_one][:, order_one])
    couplings = stack_pair(coupling, coupling_other, upper_half)[:, order_one]
    panels = panel_solve(factor_one, couplings)
    own_panel = jnp.where(upper_half, panels[:inner_rows], panels[inner_rows:])
    reduced = place_side(own_block, upper_half) - gram_rows(own_panel, panels)
    half_rows = SEP // 2
    first_factor = jnp.where(upper_half, factor_one[:half_rows], factor_one[half_rows:])
    pivot_piece = jnp.concatenate(
        [reduced[:SEP, :SEP], reduced[:SEP, inner_rows : inner_rows + SEP]], axis=1
    )
    coupling_two = jnp.concatenate(
        [reduced[SEP:, :SEP], reduced[SEP:, inner_rows : inner_rows + SEP]], axis=1
    )
    keep_block = jnp.concatenate(
        [reduced[SEP:, SEP:inner_rows], reduced[SEP:, inner_rows + SEP :]], axis=1
    )
    order_two = order_second[pair_row, pair_col]
    piece_other = partner(pivot_piece, "gx", row_bit)
    pivot_side = stack_pair(pivot_piece, piece_other, upper_half)
    side_other = partner(pivot_side, "gy", col_bit)
    pivot_two = pivot_side + side_other
    factor_two = jnp.linalg.cholesky(pivot_two[order_two][:, order_two])
    own_second = panel_solve(factor_two, coupling_two[:, order_two])
    panel_other = partner(own_second, "gx", row_bit)
    panel_side = stack_pair(own_second, panel_other, upper_half)
    panel_far = partner(panel_side, "gy", col_bit)
    all_second = stack_pair(panel_side, panel_far, left_half)
    merged_schur = place_side(keep_block, left_half) - gram_rows(own_second, all_second)
    corner_row = row_high * SEP
    corner_col = col_high * SEP
    second_factor = lax.dynamic_slice(factor_two, (corner_row, corner_col), (SEP, SEP))
    return (first_factor, own_panel, second_factor, own_second, merged_schur)


def solution(mesh):
    in_specs = (P("gx", "gy"), P("gx", "gy", None), P(None, "gy", None), P())
    out_specs = (P("gx", "gy"), P("gx", "gy"), P("gx", "gy"), P("gx", "gy"), P("gx", "gy"))
    return jax.shard_map(body, mesh=mesh, in_specs=in_specs, out_specs=out_specs, check_vma=False)
```

profile of v0, /device:TPU:0, one launch (start us, length us, event | category | flops | bytes accessed | tf_op | source)
XLA Modules:
  0.0 465.4 jit_solution(9493411079303946444)
XLA Ops:
  1.4 4.3 scatter_custom_fusion
  5.7 8.5 %gather_fusion = f32[1024,1024]{1,0:T(8,128)} fusion(f32[1024,1024]{1,0:T(8,128)} %param.6, s32[1024]{0:T(1024)S(1)} %fusion.54), kind=kCustom, calls=%fused_computation | custom fusion | bytes 8392704 | tf_op jit(solution)/shard_map/gather | solution.py:35
  14.3 5.3 %copy.21 = f32[1024,1024]{0,1:T(8,128)} copy(f32[1024,1024]{1,0:T(8,128)} %gather_fusion) | data formatting | bytes 8388608 | tf_op jit(solution)/shard_map/gather | solution.py:35
  19.6 8.5 %gather_fusion.1 = f32[1024,1024]{1,0:T(8,128)} fusion(f32[1024,1024]{0,1:T(8,128)} %copy.21, s32[1024]{0:T(1024)S(1)} %fusion.54), kind=kCustom, calls=%fused_computation.1 | custom fusion | bytes 8392704 | tf_op jit(solution)/shard_map/gather | solution.py:35
  28.1 5.5 %copy.22 = f32[1024,1024]{0,1:T(8,128)} copy(f32[1024,1024]{1,0:T(8,128)} %gather_fusion.1) | data formatting | bytes 8388608 | tf_op jit(solution)/shard_map/gather | solution.py:35
  34.6 3.0 collective-permute-start
  39.0 3.2 slice.227
  42.2 2.6 collective-permute-done
  48.0 11.7 %cholesky.135 = f32[128,128]{1,0:T(8,128)S(1)} custom-call(f32[128,128]{1,0:T(8,128)S(1)} %cholesky.339), custom_call_target="Cholesky" | custom-call | tf_op jit(solution)/shard_map/jit(cholesky)/cholesky | solution.py:90
  59.8 9.8 %custom-call.42 = f32[1,128,128]{1,2,0:T(8,128)S(1)} custom-call(f32[1,128,128]{2,1,0:T(8,128)S(1)} %get-tuple-element.75), custom_call_target="InvertDiagBlocksLowerTriangular" | custom-call | tf_op jit(solution)/shard_map/jit(cholesky)/cholesky/custom-call.1 | solution.py:90
  70.1 11.7 %cholesky.145 = f32[128,128]{1,0:T(8,128)S(1)} custom-call(f32[128,128]{1,0:T(8,128)S(1)} %convolution_subtract_fusion.6), custom_call_target="Cholesky" | custom-call | tf_op jit(solution)/shard_map/jit(cholesky)/cholesky | solution.py:90
  84.6 4.0 while.2
  85.2 1.4 bitcast_dynamic-update-slice_fusion.4
  87.2 1.4 bitcast_dynamic-update-slice_fusion.4
  88.6 20.1 %custom-call.37 = f32[2,128,128]{1,2,0:T(8,128)S(1)} custom-call(f32[2,128,128]{2,1,0:T(8,128)S(1)} %get-tuple-element.13), custom_call_target="InvertDiagBlocksLowerTriangular" | custom-call | tf_op jit(solution)/shard_map/triangular_solve | solution.py:45
  108.7 1.5 maximum_select_fusion.4
  115.3 4.1 select_subtract_fusion
  119.5 2.1 copy-done
  121.7 2.1 collective-permute-start.2
  123.8 10.2 %collective-permute-done.2 = f32[256,512]{1,0:T(8,128)S(1)} collective-permute-done((f32[256,512]{1,0:T(8,128)S(1)}, f32[256,512]{1,0:T(8,128)S(1)}, u32[]{:S(2)}, u32[]{:S(2)}) %collective-permute-start.2) | collective-permute-done | bytes 524320 | tf_op jit(solution)/shard_map/ppermute | solution.py:19
  134.1 2.6 collective-permute-start.3
  139.8 1.6 copy.30
  141.4 2.3 gather_fusion.7
  143.7 36.5 %collective-permute-done.3 = f32[512,512]{1,0:T(8,128)} collective-permute-done((f32[512,512]{1,0:T(8,128)S(1)}, f32[512,512]{1,0:T(8,128)}, u32[]{:S(2)}, u32[]{:S(2)}) %collective-permute-start.3) | collective-permute-done | bytes 1048608 | tf_op jit(solution)/shard_map/ppermute | solution.py:19
  180.2 1.4 add.163
  181.7 1.6 gather_fusion.5
  183.6 1.8 gather_fusion.6
  187.0 11.7 %cholesky.276 = f32[128,128]{1,0:T(8,128)S(1)} custom-call(f32[128,128]{1,0:T(8,128)S(1)} %cholesky.342), custom_call_target="Cholesky" | custom-call | tf_op jit(solution)/shard_map/jit(cholesky)/cholesky | solution.py:111
  199.5 9.8 %custom-call.38 = f32[1,128,128]{1,2,0:T(8,128)S(1)} custom-call(f32[1,128,128]{2,1,0:T(8,128)S(1)} %get-tuple-element.71), custom_call_target="InvertDiagBlocksLowerTriangular" | custom-call | tf_op jit(solution)/shard_map/jit(cholesky)/cholesky | solution.py:111
  211.9 11.7 %cholesky.294 = f32[128,128]{1,0:T(8,128)S(1)} custom-call(f32[128,128]{1,0:T(8,128)S(1)} %cholesky.346), custom_call_target="Cholesky" | custom-call | tf_op jit(solution)/shard_map/jit(cholesky)/cholesky | solution.py:111
  224.2 10.2 %custom-call.39 = f32[1,128,128]{1,2,0:T(8,128)S(1)} custom-call(f32[1,128,128]{2,1,0:T(8,128)S(1)} %get-tuple-element.68), custom_call_target="InvertDiagBlocksLowerTriangular" | custom-call | tf_op jit(solution)/shard_map/jit(cholesky)/cholesky | solution.py:111
  236.0 11.7 %cholesky.315 = f32[128,128]{1,0:T(8,128)S(1)} custom-call(f32[128,128]{1,0:T(8,128)S(1)} %cholesky.351), custom_call_target="Cholesky" | custom-call | tf_op jit(solution)/shard_map/jit(cholesky)/cholesky | solution.py:111
  248.4 9.8 %custom-call.43 = f32[1,128,128]{1,2,0:T(8,128)S(1)} custom-call(f32[1,128,128]{2,1,0:T(8,128)S(1)} %get-tuple-element.65), custom_call_target="InvertDiagBlocksLowerTriangular" | custom-call | tf_op jit(solution)/shard_map/jit(cholesky)/cholesky/custom-call.1 | solution.py:111
  259.7 11.7 %cholesky.328 = f32[128,128]{1,0:T(8,128)S(1)} custom-call(f32[128,128]{1,0:T(8,128)S(1)} %convolution_subtract_fusion.7), custom_call_target="Cholesky" | custom-call | tf_op jit(solution)/shard_map/jit(cholesky)/cholesky | solution.py:111
  274.7 1.7 fusion.10
  276.4 11.6 %while.3 = (s32[]{:T(128)}, f32[512,512]{1,0:T(8,128)}, s32[4,2]{0,1:T(2,128)S(1)}, f32[4,128,128]{2,1,0:T(8,128)S(1)}, s32[]{:T(128)}) while((s32[]{:T(128)}, f32[512,512]{1,0:T(8,128)}, s32[4,2]{0,1:T(2,128)S(1)}, f32[4,128,128]{2,1,0:T(8,128)S(1)}, s32[]{:T(128)}) %tuple.59), condition=%wide.while_cond.1, body=%wide.while_body.1.sunk | while | flops 2 | bytes 131189 | solution.py:45
  277.0 2.3 bitcast_dynamic-update-slice_fusion.5
  279.9 2.3 bitcast_dynamic-update-slice_fusion.5
  282.8 2.3 bitcast_dynamic-update-slice_fusion.5
  285.7 2.2 bitcast_dynamic-update-slice_fusion.5
  288.0 39.3 %custom-call.40 = f32[4,128,128]{1,2,0:T(8,128)S(1)} custom-call(f32[4,128,128]{2,1,0:T(8,128)S(1)} %get-tuple-element.21), custom_call_target="InvertDiagBlocksLowerTriangular" | custom-call | tf_op jit(solution)/shard_map/triangular_solve | solution.py:45
  331.1 1.6 convolution_subtract_fusion.3
  334.1 23.9 %collective-permute-done.4 = f32[512,512]{0,1:T(8,128)S(1)} collective-permute-done((f32[512,512]{0,1:T(8,128)S(1)}, f32[512,512]{0,1:T(8,128)S(1)}, u32[]{:S(2)}, u32[]{:S(2)}) %collective-permute-start.4) | collective-permute-done | bytes 1048608 | tf_op jit(solution)/shard_map/ppermute | solution.py:19
  358.0 1.8 maximum_select_fusion.3
  361.6 2.7 fusion.64
  365.7 1.8 dynamic_slice.11
  367.4 84.8 %collective-permute-done.5 = f32[1024,512]{0,1:T(8,128)} collective-permute-done((f32[1024,512]{0,1:T(8,128)}, f32[1024,512]{0,1:T(8,128)}, u32[]{:S(2)}, u32[]{:S(2)}) %collective-permute-start.5) | collective-permute-done | bytes 2097184 | tf_op jit(solution)/shard_map/ppermute | solution.py:19
  452.5 12.8 %fusion = f32[512,2048]{1,0:T(8,128)} fusion(f32[512,1024]{1,0:T(8,128)S(1)} %broadcast_in_dim.39, f32[512,512]{1,0:T(8,128)S(1)} %copy-done.5, f32[512,512]{1,0:T(8,128)S(1)} %get-tuple-element.56, pred[]{:T(512)S(6)} %lt.74, f32[1024,512]{0,1:T(8,128)} %collective-permute-done.5, f32[1024,512]{0,1:T(8,128)} %maximum_select_fusion.3, ...), kind=kOutput, calls=%fused_computation.15 | convolution fusion | flops 6452674560 | bytes 13631489 | tf_op jit(solution)/shard_map/ik,jk->ij/dot_general | solution.py:39
  (101 shorter events, 38.9 us)
Async XLA Ops:
  34.6 10.2 %collective-permute-start = (f32[256,256]{1,0:T(8,128)S(1)}, f32[256,256]{1,0:T(8,128)S(1)}, u32[]{:S(2)}, u32[]{:S(2)}) collective-permute-start(f32[256,256]{1,0:T(8,128)S(1)} %slice.219), channel_id=1, source_target_pairs={{0,16},{16,0},{8,24},{24,8},{1,17},{17,1},{9,25},{25,9},{2,18},{18... | collective-permute-start | bytes 786440 | tf_op jit(solution)/shard_map/ppermute | solution.py:19
  38.8 69.9 %collective-permute-start.1 = (f32[768,256]{1,0:T(8,128)S(1)}, f32[768,256]{1,0:T(8,128)}, u32[]{:S(2)}, u32[]{:S(2)}) collective-permute-start(f32[768,256]{1,0:T(8,128)S(1)} %slice.222), channel_id=1, source_target_pairs={{0,16},{16,0},{8,24},{24,8},{1,17},{17,1},{9,25},{25,9},{2,18},{18... | collective-permute-start | bytes 2359304 | tf_op jit(solution)/shard_map/ppermute | solution.py:19
  38.9 3.2 copy-start.6
  113.7 1.7 copy-start.1
  119.4 2.1 copy-start
  121.7 12.4 %collective-permute-start.2 = (f32[256,512]{1,0:T(8,128)S(1)}, f32[256,512]{1,0:T(8,128)S(1)}, u32[]{:S(2)}, u32[]{:S(2)}) collective-permute-start(f32[256,512]{1,0:T(8,128)S(1)} %pad_maximum_fusion.4), channel_id=1, source_target_pairs={{0,16},{16,0},{8,24},{24,8},{1,17},{17,1},{9,25},{25,9},{2,18},{18... | collective-permute-start | bytes 1572872 | tf_op jit(solution)/shard_map/ppermute | solution.py:19
  134.1 46.1 %collective-permute-start.3 = (f32[512,512]{1,0:T(8,128)S(1)}, f32[512,512]{1,0:T(8,128)}, u32[]{:S(2)}, u32[]{:S(2)}) collective-permute-start(f32[512,512]{1,0:T(8,128)S(1)} %maximum_select_fusion.7), channel_id=1, source_target_pairs={{0,4},{4,0},{1,5},{5,1},{2,6},{6,2},{3,7},{7,3},{8,12},{12,8},{9,1... | collective-permute-start | bytes 3145736 | tf_op jit(solution)/shard_map/ppermute | solution.py:19
  186.0 1.0 copy-start.3
  259.7 67.6 %copy-start.2 = (f32[512,512]{1,0:T(8,128)S(1)}, f32[512,512]{1,0:T(8,128)}, u32[]{:S(2)}) copy-start(f32[512,512]{1,0:T(8,128)} %gather_fusion.7) | copy-start | bytes 3145732
  333.2 26.6 %copy-start.4 = (f32[256,256]{1,0:T(8,128)S(1)}, f32[256,256]{1,0:T(8,128)}, u32[]{:S(2)}) copy-start(f32[256,256]{1,0:T(8,128)} %get-tuple-element.51) | copy-start | bytes 786436
  333.2 24.8 %collective-permute-start.4 = (f32[512,512]{0,1:T(8,128)S(1)}, f32[512,512]{0,1:T(8,128)S(1)}, u32[]{:S(2)}, u32[]{:S(2)}) collective-permute-start(f32[512,512]{0,1:T(8,128)S(1)} %pad_maximum_fusion.3), channel_id=1, source_target_pairs={{0,16},{16,0},{8,24},{24,8},{1,17},{17,1},{9,25},{25,9},{2,18},{18... | collective-permute-start | bytes 3145736 | tf_op jit(solution)/shard_map/ppermute | solution.py:19
  359.8 92.4 %collective-permute-start.5 = (f32[1024,512]{0,1:T(8,128)}, f32[1024,512]{0,1:T(8,128)}, u32[]{:S(2)}, u32[]{:S(2)}) collective-permute-start(f32[1024,512]{0,1:T(8,128)} %maximum_select_fusion.3), channel_id=1, source_target_pairs={{0,4},{4,0},{1,5},{5,1},{2,6},{6,2},{3,7},{7,3},{8,12},{12,8},{9,1... | collective-permute-start | bytes 6291464 | tf_op jit(solution)/shard_map/ppermute | solution.py:19
  365.7 86.8 %copy-start.5 = (f32[512,512]{1,0:T(8,128)S(1)}, f32[512,512]{1,0:T(8,128)}, u32[]{:S(2)}) copy-start(f32[512,512]{1,0:T(8,128)} %get-tuple-element.57) | copy-start | bytes 3145732
where the time goes:
time: 470 us; the launch traced here: 465 us
  other arithmetic  185 us (39%)
  waiting for transfers between devices  158 us (34%)
  local copies, waits for them, and re-layouts  77.5 us (16%)
  matrix products  31.1 us (7%)
  starting transfers between devices  8.67 us (2%)
  between operations  5.29 us (1%)
    ppermute x6, waiting for transfers between devices, partner(): return lax.ppermute(block, axis, route)  158 us
    another operation x15, other arithmetic, body(): factor_two = jnp.linalg.cholesky(pivot_two[order_two][:, order_two])  79.4 us
    another operation x7, other arithmetic, panel_solve(): lax.linalg.triangular_solve(factor, coupling, left_side=False, lower=True...  62 us
    another operation x6, other arithmetic, body(): factor_one = jnp.linalg.cholesky(pivot_one[order_one][:, order_one])  34 us
    gather x4, local copies, waits for them, and re-layouts, reorder(): return sub_block[inverse][:, inverse]  27.9 us
    dot_general x2, matrix products, gram_rows(): jnp.einsum('ik,jk->ij', left_rows, right_rows, precision=highest, preferr...  16.8 us
    another operation x18, local copies, waits for them, and re-layouts  15.4 us
  transfers between devices with their start and end apart: 6, of which 5 were waited for; matrix products, arithmetic and copies ran while one was open for 18% of the time, Pallas kernels for 0%

commit v1 on v0

v1 whole, which is shorter than its diff:
```python
import jax
import jax.numpy as jnp
from jax import lax
from jax.experimental import pallas as pl
from jax.experimental.pallas import tpu as pltpu
from jax.sharding import PartitionSpec as P

SEP = 256

STEP = 64


def halves(x):
    high = x.astype(jnp.bfloat16)
    low = (x - high.astype(jnp.float32)).astype(jnp.bfloat16)
    return high, low


def mm(a, b, dims):
    return lax.dot_general(a, b, (dims, ((), ())), preferred_element_type=jnp.float32)


def mm3(a, b, dims):
    a_high, a_low = halves(a)
    b_high, b_low = halves(b)
    return mm(a_high, b_high, dims) + (mm(a_high, b_low, dims) + mm(a_low, b_high, dims))


def eliminate(tiles):
    count = len(tiles)
    sub = lax.broadcasted_iota(jnp.int32, (8, 128), 0)
    for t in range(count):
        cols = {
            g: [jnp.broadcast_to(tiles[g][:, 8 * t + k : 8 * t + k + 1], (8, 128)) for k in range(8)]
            for g in range(t, count)
        }
        for k in range(8):
            scale = lax.rsqrt(cols[t][k][k : k + 1, :])
            final_row = tiles[t][k : k + 1, :] * scale
            diag_row = [cols[t][m][k : k + 1, :] * scale for m in range(k + 1, 8)]
            for g in range(t, count):
                factor = cols[g][k] * scale
                if g == t:
                    factor = jnp.where(sub > k, factor, 0.0)
                for m in range(k + 1, 8):
                    cols[g][m] = cols[g][m] - factor * diag_row[m - k - 1]
                tiles[g] = tiles[g] - factor * final_row
            tiles[t] = jnp.where(sub == k, final_row, tiles[t])
    return tiles


def chol_kernel(q_ref, order_ref, lower_ref, inv_ref, work):
    n = q_ref.shape[0]
    pick = (order_ref[...] == lax.broadcasted_iota(jnp.int32, (n, n), 1)).astype(jnp.float32)
    pick16 = pick.astype(jnp.bfloat16)
    q_high, q_low = halves(q_ref[...])
    rows = mm(pick16, q_high, ((1,), (0,))) + mm(pick16, q_low, ((1,), (0,)))
    r_high, r_low = halves(rows)
    work[:, :n] = mm(r_high, pick16, ((1,), (1,))) + mm(r_low, pick16, ((1,), (1,)))
    work[:, n:] = pick
    lane = lax.broadcasted_iota(jnp.int32, (STEP, 128), 1)
    eye = jnp.where(
        lane == lax.broadcasted_iota(jnp.int32, (STEP, 128), 0) + STEP, 1.0, 0.0
    )

    def panel(p, carry):
        start = pl.multiple_of(p * STEP, STEP)
        base = pl.multiple_of((p // 2) * 128, 128)
        block = work[pl.ds(start, STEP), pl.ds(base, 128)]
        block = jnp.where(p % 2 == 0, block, pltpu.roll(block, STEP, 1))
        block = jnp.where(lane < STEP, block, eye)
        tiles = eliminate([block[8 * g : 8 * g + 8, :] for g in range(STEP // 8)])
        inverse = jnp.concatenate(tiles, axis=0)[:, STEP:]
        strip = mm3(inverse, work[pl.ds(start, STEP), :], ((1,), (0,)))
        work[pl.ds(start, STEP), :] = strip
        s_high, s_low = halves(strip)
        column = lax.broadcasted_iota(jnp.int32, (STEP, n), 1)
        after = column >= start + STEP
        c_high, c_low = halves(jnp.where(after, strip[:, :n], 0.0))
        left = jnp.concatenate([c_high, c_high, c_low, c_low], axis=0)
        right = jnp.concatenate([s_high, s_low, s_high, s_low], axis=0)
        work[...] -= mm(left, right, ((0,), (0,)))
        return carry

    lax.fori_loop(0, n // STEP, panel, 0)
    row = lax.broadcasted_iota(jnp.int32, (n, n), 0)
    col = lax.broadcasted_iota(jnp.int32, (n, n), 1)
    lower_ref[...] = jnp.where(row <= col, work[:, :n], 0.0).T
    inv_ref[...] = work[:, n:]


def chol(q, order):
    n = q.shape[0]
    spec = pl.BlockSpec(memory_space=pltpu.VMEM)
    return pl.pallas_call(
        chol_kernel,
        out_shape=(jax.ShapeDtypeStruct((n, n), jnp.float32),) * 2,
        in_specs=[spec, spec],
        out_specs=(spec, spec),
        scratch_shapes=[pltpu.VMEM((n, 2 * n), jnp.float32)],
        compiler_params=pltpu.CompilerParams(vmem_limit_bytes=40 << 20),
        cost_estimate=pl.CostEstimate(flops=n * 60_000_000, bytes_accessed=12 * n * n, transcendentals=0),
    )(q, order.reshape(n, 1))


def reorder_kernel(row_ranks, col_count, a_ref, row_ref, col_ref, out_ref):
    n = a_ref.shape[0]
    rows = lax.broadcasted_iota(jnp.int32, (SEP, n), 0)
    picked = [jnp.where(rows + rank * SEP == row_ref[...], 1.0, 0.0) for rank in row_ranks]
    pick = jnp.concatenate(picked, axis=0).astype(jnp.bfloat16)
    a_high, a_low = halves(a_ref[...])
    moved = mm(pick, a_high, ((1,), (0,))) + mm(pick, a_low, ((1,), (0,)))
    m_high, m_low = halves(moved)
    cols = lax.broadcasted_iota(jnp.int32, (n, col_count), 1)
    spread = jnp.where(cols == col_ref[...], 1.0, 0.0).astype(jnp.bfloat16)
    out_ref[...] = mm(m_high, spread, ((1,), (0,))) + mm(m_low, spread, ((1,), (0,)))


def reorder(sub_block, target, row_ranks, col_count):
    n = sub_block.shape[0]
    spec = pl.BlockSpec(memory_space=pltpu.VMEM)
    rows = len(row_ranks) * SEP
    return pl.pallas_call(
        lambda *refs: reorder_kernel(row_ranks, col_count, *refs),
        out_shape=jax.ShapeDtypeStruct((rows, col_count), jnp.float32),
        in_specs=[spec, spec, spec],
        out_specs=spec,
        compiler_params=pltpu.CompilerParams(vmem_limit_bytes=40 << 20),
        cost_estimate=pl.CostEstimate(
            flops=4 * rows * n * (n + col_count), bytes_accessed=4 * n * n, transcendentals=0
        ),
    )(sub_block, target.reshape(1, n), target.reshape(n, 1))


def partner(block, axis, stride):
    count = lax.axis_size(axis)
    route = []
    for low in range(count):
        high = low | 1 << stride
        if high != low and high < count:
            route += [(low, high), (high, low)]
    return lax.ppermute(block, axis, route)


def after(value, *others):
    return lax.optimization_barrier((value, *others))[0]


def high_dot(a, b, dims):
    return lax.dot_general(
        a, b, (dims, ((), ())), precision=lax.Precision.HIGH, preferred_element_type=jnp.float32
    )


def new_targets(slots, left_side, upper_side):
    edge_index = slots // SEP
    west_pos = jnp.where(left_side, 1, 0).astype(jnp.int32)
    north_pos = jnp.where(upper_side, 2, 3).astype(jnp.int32)
    new_edge = jnp.where(
        edge_index == 0,
        west_pos,
        jnp.where(
            edge_index == 1, 1 - west_pos, jnp.where(edge_index == 2, north_pos, 5 - north_pos)
        ),
    )
    return new_edge * SEP + slots % SEP


def body(local_schur, boundary_map, order_first, order_second):
    row_count = lax.axis_size("gx")
    col_count = lax.axis_size("gy")
    row_bit = row_count.bit_length() - 2
    col_bit = col_count.bit_length() - 2
    pair_rows = row_count // 2
    pair_cols = col_count // 2
    row_index = lax.axis_index("gx")
    col_index = lax.axis_index("gy")
    upper = row_index < pair_rows
    left = col_index < pair_cols
    row_high = row_index // pair_rows
    col_high = col_index // pair_cols
    own_slot = 2 * col_high + row_high
    pair_row = row_index % pair_rows
    pair_col = col_index % pair_cols

    def row_swap(block):
        return partner(block, "gx", row_bit)

    def col_swap(block):
        return partner(block, "gy", col_bit)

    target = new_targets(boundary_map[0, 0], left, upper)
    first = reorder(local_schur, target, (0, 3), 4 * SEP)
    corner = first[:SEP, :SEP]
    shared = first[SEP:, 3 * SEP :]
    coupling = first[SEP:, : 3 * SEP]
    shared_other = row_swap(shared)
    corner_far = col_swap(corner)
    outer = reorder(local_schur, target, (1, 2), 3 * SEP)
    raw = outer[:, :SEP]
    keep = outer[:, SEP:]
    coupling_other = row_swap(after(coupling, shared_other))
    raw_half = col_swap(after(raw[:SEP], corner_far))
    corner_sum = corner + corner_far
    corner_other = row_swap(after(corner_sum, coupling_other))

    factor_one, inverse_one = chol(shared + shared_other, order_first[pair_row, 0])
    first_factor = jnp.where(upper, factor_one[: SEP // 2], factor_one[SEP // 2 :])
    own_panel = high_dot(coupling, inverse_one, ((0,), (1,)))
    own_inner = own_panel[:SEP]
    own_outer = own_panel[SEP:]
    inner_far = col_swap(own_inner)
    other_panel = high_dot(coupling_other, inverse_one, ((0,), (1,)))
    other_inner = other_panel[:SEP]
    other_outer = other_panel[SEP:]
    inner_far_other = row_swap(inner_far)

    keep_own = keep - high_dot(own_outer, own_outer, ((1,), (1,)))
    keep_other = -high_dot(own_outer, other_outer, ((1,), (1,)))
    base = jnp.zeros((2 * SEP, 8 * SEP), jnp.float32)
    base = lax.dynamic_update_slice(base, keep_own, (0, own_slot * 2 * SEP))
    base = lax.dynamic_update_slice(base, keep_other, (0, (own_slot ^ 1) * 2 * SEP))

    outer_far = col_swap(after(own_outer, inner_far))
    raw_rest = col_swap(after(raw[SEP:], inner_far, outer_far))
    raw_other = row_swap(after(raw, inner_far_other))

    def stack(own_part, other_part):
        return jnp.concatenate(
            [jnp.where(upper, own_part, other_part), jnp.where(upper, other_part, own_part)], axis=0
        )

    side_own = stack(own_inner, other_inner)
    side_far = stack(inner_far, inner_far_other)
    sides = jnp.concatenate([side_own, side_far], axis=1)
    zero = jnp.zeros((SEP, SEP), jnp.float32)
    corner_up = jnp.where(upper, corner_sum, corner_other)
    corner_low = jnp.where(upper, corner_other, corner_sum)
    placed = jnp.concatenate(
        [
            jnp.concatenate([corner_up, zero], axis=1),
            jnp.concatenate([zero, corner_low], axis=1),
        ],
        axis=0,
    )
    pivot_two = placed - high_dot(sides, sides, ((1,), (1,)))
    factor_two, inverse_two = chol(pivot_two, order_second[pair_row, pair_col])
    second_factor = lax.dynamic_slice(factor_two, (row_high * SEP, col_high * SEP), (SEP, SEP))

    raw_far = jnp.concatenate([raw_half, raw_rest], axis=0)
    raw_far_other = row_swap(raw_far)
    outer_far_other = row_swap(outer_far)

    inner_maps = high_dot(inverse_two, sides, ((1,), (0,)))
    map_own = -inner_maps[:, :SEP]
    map_far = -inner_maps[:, SEP:]
    half_own = jnp.where(upper, inverse_two[:, :SEP], inverse_two[:, SEP:])
    half_other = jnp.where(upper, inverse_two[:, SEP:], inverse_two[:, :SEP])

    def second(raw_part, outer_part, half, inner_map):
        return high_dot(
            jnp.concatenate([raw_part, outer_part], axis=1),
            jnp.concatenate([half, inner_map], axis=1),
            ((1,), (1,)),
        )

    second_own = second(raw, own_outer, half_own, map_own)
    local = jnp.stack(
        [
            second_own,
            second(raw_other, other_outer, half_other, map_own),
            second(raw_far, outer_far, half_own, map_far),
            second(raw_far_other, outer_far_other, half_other, map_far),
        ]
    )
    every = jnp.concatenate(
        [lax.dynamic_index_in_dim(local, slot ^ own_slot, 0, keepdims=False) for slot in range(4)],
        axis=0,
    )
    merged_schur = base - high_dot(second_own, every, ((1,), (1,)))
    return (first_factor, own_panel, second_factor, second_own, merged_schur)


def solution(mesh):
    in_specs = (P("gx", "gy"), P("gx", "gy", None), P(None, "gy", None), P())
    out_specs = (P("gx", "gy"), P("gx", "gy"), P("gx", "gy"), P("gx", "gy"), P("gx", "gy"))
    return jax.shard_map(body, mesh=mesh, in_specs=in_specs, out_specs=out_specs, check_vma=False)
```

time: 470 us -> 132 us (0.28)
  other arithmetic: 185 us -> 3.82 us
  waiting for transfers between devices: 158 us -> 46.8 us
  local copies, waits for them, and re-layouts: 77.5 us -> 12.3 us
  Pallas kernels: 0 us -> 39.9 us
  matrix products: 31.1 us -> 15.4 us
    another operation x28 -> x1, other arithmetic: 175 us -> 0.54 us  [body(): jnp.stack([second_own, second(raw_other, other_outer, half_other, map_own...]
    ppermute x6 -> x12, waiting for transfers between devices: 158 us -> 46.8 us  [partner(): return lax.ppermute(block, axis, route)]
    pallas_call x0 -> x4, Pallas kernels: none -> 39.9 us  [the longest x2 30.4 us: chol(): pl.pallas_call(chol_kernel, out_shape=(jax.ShapeDtypeStruct((n, n), jnp.f...]
    gather x14 -> x0, local copies, waits for them, and re-layouts: 37.8 us -> none  [the longest x4 27.9 us: reorder(): return sub_block[inverse][:, inverse]]
    another operation x26 -> x4, local copies, waits for them, and re-layouts: 15.7 us -> 0.3 us  [chol(): order.reshape(n, 1)]
    another operation x18 -> x0, matrix products: 14.3 us -> none  [the longest x10 8.33 us: panel_solve(): lax.linalg.triangular_solve(factor, coupling, left_side=False, lower=True...]
    slice x6 -> x7, local copies, waits for them, and re-layouts: 9.44 us -> 3.89 us  [the longest x1 1.08 us: body(): raw = outer[:, :SEP]]
    select_n x8 -> x4, other arithmetic: 5.62 us -> 0.81 us  [the longest x1 0.67 us: body(): jnp.where(upper, factor_one[:SEP // 2], factor_one[SEP // 2:])]
  transfers between devices with their start and end apart: 6 -> 12, of which waited for: 5 -> 7; matrix products, arithmetic and copies ran while one was open for 18% -> 11% of each run, Pallas kernels for 0% -> 27%
where the time goes in v1:
time: 132 us
  waiting for transfers between devices  46.8 us (35%)
  Pallas kernels  39.9 us (30%)
  matrix products  15.4 us (12%)
  starting transfers between devices  12.4 us (9%)
  local copies, waits for them, and re-layouts  12.3 us (9%)
  other arithmetic  3.82 us (3%)
    ppermute x12, waiting for transfers between devices, partner(): return lax.ppermute(block, axis, route)  46.8 us
    pallas_call x2, Pallas kernels, chol(): pl.pallas_call(chol_kernel, out_shape=(jax.ShapeDtypeStruct((n, n), jnp.f...  30.4 us
    dot_general x11, matrix products, high_dot(): lax.dot_general(a, b, (dims, ((), ())), precision=lax.Precision.HIGH, pre...  15.4 us
    ppermute x12, starting transfers between devices, partner(): return lax.ppermute(block, axis, route)  12.4 us
    pallas_call x2, Pallas kernels, reorder(): pl.pallas_call(lambda *refs: reorder_kernel(row_ranks, col_count, *refs),...  9.55 us
    unnamed x19, local copies, waits for them, and re-layouts  5.56 us
  transfers between devices with their start and end apart: 12, of which 7 were waited for; matrix products, arithmetic and copies ran while one was open for 11% of the time, Pallas kernels for 27%

profile of v1, /device:TPU:0, one launch (start us, length us, event | category | flops | bytes accessed | tf_op | source)
XLA Modules:
  0.0 131.7 jit_solution(10751443024976829796)
XLA Ops:
  0.7 0.9 copy.11
  1.6 0.7 fusion.29.refs_1_
  2.3 0.6 fusion.27.refs_2_
  2.9 2.2 %copy-done.3 = f32[1024,1024]{1,0:T(8,128)S(1)} copy-done((f32[1024,1024]{1,0:T(8,128)S(1)}, f32[1024,1024]{1,0:T(8,128)}, u32[]{:S(2)}) %copy-start.3) | copy-done | bytes 4194328
  5.1 4.8 %shard_map.83 = f32[512,1024]{1,0:T(8,128)S(1)} custom-call(f32[1024,1024]{1,0:T(8,128)S(1)} %copy-done.3, s32[1,1024]{1,0:T(1,128)S(1)} %fusion.29.refs_1_, s32[1024,1]{1,0:T(8,128)S(1)} %fusion.27.refs_2_), custom_call_target="tpu_custom_call" | custom-call | flops 4294967296 | bytes 4194304 | tf_op jit(solution)/shard_map/pallas_call | solution.py:123
  9.9 0.8 fusion.44
  10.6 4.0 %collective-permute-start.1 = (f32[256,256]{1,0:T(8,128)S(1)}, f32[256,256]{1,0:T(8,128)S(1)}, u32[]{:S(2)}, u32[]{:S(2)}) collective-permute-start(f32[256,256]{1,0:T(8,128)S(1)} %get-tuple-element.31), channel_id=1, source_target_pairs={{0,4},{4,0},{1,5},{5,1},{2,6},{6,2},{3,7},{7,3},{8,12},{12,8},{9,1... | collective-permute-start | bytes 786440 | tf_op jit(solution)/shard_map/ppermute | solution.py:142
  14.7 1.5 %collective-permute-start = (f32[256,256]{1,0:T(8,128)}, f32[256,256]{1,0:T(8,128)}, u32[]{:S(2)}, u32[]{:S(2)}) collective-permute-start(f32[256,256]{1,0:T(8,128)} %get-tuple-element.32), channel_id=1, source_target_pairs={{0,16},{16,0},{8,24},{24,8},{1,17},{17,1},{9,25},{25,9},{2,18},{18... | collective-permute-start | bytes 786440 | tf_op jit(solution)/shard_map/ppermute | solution.py:142
  16.2 2.2 %copy-done.4 = f32[1024,1024]{1,0:T(8,128)S(1)} copy-done((f32[1024,1024]{1,0:T(8,128)S(1)}, f32[1024,1024]{1,0:T(8,128)}, u32[]{:S(2)}) %copy-start.4) | copy-done | bytes 4194328
  18.4 4.8 %shard_map.86 = f32[512,768]{1,0:T(8,128)S(1)} custom-call(f32[1024,1024]{1,0:T(8,128)S(1)} %copy-done.4, s32[1,1024]{1,0:T(1,128)S(1)} %fusion.29.refs_1_, s32[1024,1]{1,0:T(8,128)S(1)} %fusion.27.refs_2_), custom_call_target="tpu_custom_call" | custom-call | flops 3758096384 | bytes 4194304 | tf_op jit(solution)/shard_map/pallas_call | solution.py:123
  23.2 1.1 copy-done.1
  24.3 0.9 slice.73
  25.4 0.1 copy.16.order_ref
  25.6 1.1 slice.77
  26.7 1.1 fusion.45
  27.8 0.6 collective-permute-start.2
  28.4 1.0 slice_add_fusion
  29.4 9.4 %shard_map.84 = (f32[256,256]{1,0:T(8,128)S(1)}, f32[256,256]{1,0:T(8,128)S(1)}) custom-call(f32[256,256]{1,0:T(8,128)S(1)} %get-tuple-element.30.q_ref, s32[256,1]{1,0:T(8,128)S(1)} %copy.15.order_ref), custom_call_target="tpu_custom_call" | custom-call | flops 15360000000 | bytes 786432 | tf_op jit(solution)/shard_map/pallas_call | solution.py:95
  38.8 0.8 fusion.40
  39.7 0.5 broadcast_in_dim.35
  40.2 0.7 fusion.12
  40.9 5.9 %collective-permute-done.2 = f32[256,768]{1,0:T(8,128)S(1)} collective-permute-done((f32[256,768]{1,0:T(8,128)}, f32[256,768]{1,0:T(8,128)S(1)}, u32[]{:S(2)}, u32[]{:S(2)}) %collective-permute-start.2) | collective-permute-done | bytes 786464 | tf_op jit(solution)/shard_map/ppermute | solution.py:142
  46.8 0.8 fusion.46
  47.7 0.4 collective-permute-start.4
  48.1 0.7 slice_select_fusion.4
  48.7 11.5 %collective-permute-done.7 = f32[256,256]{1,0:T(8,128)S(1)} collective-permute-done((f32[256,256]{1,0:T(8,128)S(1)}, f32[256,256]{1,0:T(8,128)S(1)}, u32[]{:S(2)}, u32[]{:S(2)}) %collective-permute-start.7) | collective-permute-done | bytes 262176 | tf_op jit(solution)/shard_map/ppermute | solution.py:142
  60.2 1.6 %collective-permute-start.3 = (f32[256,256]{1,0:T(8,128)S(1)}, f32[256,256]{1,0:T(8,128)S(1)}, u32[]{:S(2)}, u32[]{:S(2)}) collective-permute-start(f32[256,256]{1,0:T(8,128)S(1)} %get-tuple-element.18), channel_id=1, source_target_pairs={{0,16},{16,0},{8,24},{24,8},{1,17},{17,1},{9,25},{25,9},{2,18},{18... | collective-permute-start | bytes 786440 | tf_op jit(solution)/shard_map/ppermute | solution.py:142
  61.8 2.8 %collective-permute-done.4 = f32[256,256]{1,0:T(8,128)S(1)} collective-permute-done((f32[256,256]{1,0:T(8,128)S(1)}, f32[256,256]{1,0:T(8,128)S(1)}, u32[]{:S(2)}, u32[]{:S(2)}) %collective-permute-start.4) | collective-permute-done | bytes 262176 | tf_op jit(solution)/shard_map/ppermute | solution.py:142
  64.7 1.5 %collective-permute-start.5 = (f32[256,256]{1,0:T(8,128)S(1)}, f32[256,256]{1,0:T(8,128)S(1)}, u32[]{:S(2)}, u32[]{:S(2)}) collective-permute-start(f32[256,256]{1,0:T(8,128)S(1)} %collective-permute-done.4), channel_id=1, source_target_pairs={{0,16},{16,0},{8,24},{24,8},{1,17},{17,1},{9,25},{25,9},{2,18},{18... | collective-permute-start | bytes 786440 | tf_op jit(solution)/shard_map/ppermute | solution.py:142
  66.2 0.6 fusion.11
  66.9 0.2 collective-permute-done.3
  67.1 5.2 %collective-permute-done.5 = f32[256,256]{1,0:T(8,128)S(1)} collective-permute-done((f32[256,256]{1,0:T(8,128)S(1)}, f32[256,256]{1,0:T(8,128)S(1)}, u32[]{:S(2)}, u32[]{:S(2)}) %collective-permute-start.5) | collective-permute-done | bytes 262176 | tf_op jit(solution)/shard_map/ppermute | solution.py:142
  72.3 1.5 %collective-permute-start.6 = (f32[512,256]{1,0:T(8,128)S(1)}, f32[512,256]{1,0:T(8,128)S(1)}, u32[]{:S(2)}, u32[]{:S(2)}) collective-permute-start(f32[512,256]{1,0:T(8,128)S(1)} %slice.77), channel_id=1, source_target_pairs={{0,16},{16,0},{8,24},{24,8},{1,17},{17,1},{9,25},{25,9},{2,18},{18... | collective-permute-start | bytes 1572872 | tf_op jit(solution)/shard_map/ppermute | solution.py:142
  73.9 1.0 convolution_subtract_fusion.1.q_ref
  74.9 21.0 %shard_map.85 = (f32[512,512]{1,0:T(8,128)S(1)}, f32[512,512]{1,0:T(8,128)S(1)}) custom-call(f32[512,512]{1,0:T(8,128)S(1)} %convolution_subtract_fusion.1.q_ref, s32[512,1]{1,0:T(8,128)S(1)} %copy.16.order_ref), custom_call_target="tpu_custom_call" | custom-call | flops 30720000000 | bytes 3145728 | tf_op jit(solution)/shard_map/pallas_call | solution.py:95
  95.9 0.7 dynamic_slice.24
  96.6 1.0 fusion.26
  97.6 0.6 collective-permute-start.11
  98.2 11.4 %collective-permute-done.9 = f32[256,256]{1,0:T(8,128)S(1)} collective-permute-done((f32[256,256]{1,0:T(8,128)S(1)}, f32[256,256]{1,0:T(8,128)S(1)}, u32[]{:S(2)}, u32[]{:S(2)}) %collective-permute-start.9) | collective-permute-done | bytes 262176 | tf_op jit(solution)/shard_map/ppermute | solution.py:142
  109.6 0.6 collective-permute-start.10
  110.3 1.1 fusion.13
  111.4 1.0 convolution_bitcast_fusion.1
  112.5 1.1 convolution_bitcast_fusion.2
  113.5 9.9 %collective-permute-done.10 = f32[512,256]{1,0:T(8,128)S(1)} collective-permute-done((f32[512,256]{1,0:T(8,128)S(1)}, f32[512,256]{1,0:T(8,128)S(1)}, u32[]{:S(2)}, u32[]{:S(2)}) %collective-permute-start.10) | collective-permute-done | bytes 524320 | tf_op jit(solution)/shard_map/ppermute | solution.py:142
  123.4 1.0 convolution_bitcast_fusion
  124.5 0.5 pad_maximum_fusion
  125.0 0.5 dynamic-slice_bitcast_fusion.3
  125.5 6.2 %fusion.8 = f32[512,2048]{1,0:T(8,128)} fusion(f32[512,2048]{1,0:T(8,128)S(1)} %fusion.11, f32[512,512]{1,0:T(8,128)S(1)} %fusion.13, f32[512,512]{1,0:T(8,128)S(1)} %get-tuple-element.26, f32[512,512]{1,0:T(8,128)S(1)} %get-tuple-element.27, f32[512,512]{1,0:T(8,128)S(1)} %get-tuple-element.28, f32[512,512]{1,0:T(8,128)S(1)} %get-tuple-element.25), kind=kOutput, calls=%fused_computation.9 | convolution fusion | flops 3225419776 | bytes 13631488 | tf_op jit(solution)/shard_map/dot_general | solution.py:150
  (35 shorter events, 0.7 us)
Async XLA Ops:
  0.6 23.7 %copy-start = (s32[2,4,512]{2,1,0:T(4,128)S(1)}, s32[2,4,512]{2,1,0:T(4,128)}, u32[]{:S(2)}) copy-start(s32[2,4,512]{2,1,0:T(4,128)} %param.7) | copy-start | bytes 49156
  2.9 2.2 %copy-start.3 = (f32[1024,1024]{1,0:T(8,128)S(1)}, f32[1024,1024]{1,0:T(8,128)}, u32[]{:S(2)}) copy-start(f32[1024,1024]{1,0:T(8,128)} %refs_0_.3) | copy-start | bytes 12582916
  10.6 17.7 %collective-permute-start.1 = (f32[256,256]{1,0:T(8,128)S(1)}, f32[256,256]{1,0:T(8,128)S(1)}, u32[]{:S(2)}, u32[]{:S(2)}) collective-permute-start(f32[256,256]{1,0:T(8,128)S(1)} %get-tuple-element.31), channel_id=1, source_target_pairs={{0,4},{4,0},{1,5},{5,1},{2,6},{6,2},{3,7},{7,3},{8,12},{12,8},{9,1... | collective-permute-start | bytes 786440 | tf_op jit(solution)/shard_map/ppermute | solution.py:142
  14.7 13.1 %collective-permute-start = (f32[256,256]{1,0:T(8,128)}, f32[256,256]{1,0:T(8,128)}, u32[]{:S(2)}, u32[]{:S(2)}) collective-permute-start(f32[256,256]{1,0:T(8,128)} %get-tuple-element.32), channel_id=1, source_target_pairs={{0,16},{16,0},{8,24},{24,8},{1,17},{17,1},{9,25},{25,9},{2,18},{18... | collective-permute-start | bytes 786440 | tf_op jit(solution)/shard_map/ppermute | solution.py:142
  16.2 2.2 %copy-start.4 = (f32[1024,1024]{1,0:T(8,128)S(1)}, f32[1024,1024]{1,0:T(8,128)}, u32[]{:S(2)}) copy-start(f32[1024,1024]{1,0:T(8,128)} %refs_0_.3) | copy-start | bytes 12582916
  18.4 5.9 %copy-start.8 = (s32[2,1,256]{2,1,0:T(1,128)S(1)}, s32[2,1,256]{2,1,0:T(1,128)}, u32[]{:S(2)}) copy-start(s32[2,1,256]{2,1,0:T(1,128)} %param.6) | copy-start | bytes 6148
  23.1 1.1 copy-start.1
  27.8 19.0 %collective-permute-start.2 = (f32[256,768]{1,0:T(8,128)}, f32[256,768]{1,0:T(8,128)S(1)}, u32[]{:S(2)}, u32[]{:S(2)}) collective-permute-start(f32[256,768]{1,0:T(8,128)} %slice.73), channel_id=1, source_target_pairs={{0,16},{16,0},{8,24},{24,8},{1,17},{17,1},{9,25},{25,9},{2,18},{18... | collective-permute-start | bytes 2359304 | tf_op jit(solution)/shard_map/ppermute | solution.py:142
  38.8 1.5 %copy-start.2 = (f32[512,768]{1,0:T(8,128)S(1)}, f32[512,768]{1,0:T(8,128)}, u32[]{:S(2)}) copy-start(f32[512,768]{1,0:T(8,128)} %copy-done.1) | copy-start | bytes 4718596
  39.6 26.6 %copy-start.6 = (f32[768,256]{1,0:T(8,128)}, f32[768,256]{1,0:T(8,128)S(1)}, u32[]{:S(2)}) copy-start(f32[768,256]{1,0:T(8,128)S(1)} %fusion.40) | copy-start | bytes 2359300
  39.6 20.6 %collective-permute-start.7 = (f32[256,256]{1,0:T(8,128)S(1)}, f32[256,256]{1,0:T(8,128)S(1)}, u32[]{:S(2)}, u32[]{:S(2)}) collective-permute-start(f32[256,256]{1,0:T(8,128)S(1)} %get-tuple-element.22), channel_id=1, source_target_pairs={{0,4},{4,0},{1,5},{5,1},{2,6},{6,2},{3,7},{7,3},{8,12},{12,8},{9,1... | collective-permute-start | bytes 786440 | tf_op jit(solution)/shard_map/ppermute | solution.py:142
  47.6 27.3 %copy-start.7 = (f32[768,256]{1,0:T(8,128)}, f32[768,256]{1,0:T(8,128)S(1)}, u32[]{:S(2)}) copy-start(f32[768,256]{1,0:T(8,128)S(1)} %fusion.46) | copy-start | bytes 2359300
  47.7 17.0 %collective-permute-start.4 = (f32[256,256]{1,0:T(8,128)S(1)}, f32[256,256]{1,0:T(8,128)S(1)}, u32[]{:S(2)}, u32[]{:S(2)}) collective-permute-start(f32[256,256]{1,0:T(8,128)S(1)} %get-tuple-element.41), channel_id=1, source_target_pairs={{0,4},{4,0},{1,5},{5,1},{2,6},{6,2},{3,7},{7,3},{8,12},{12,8},{9,1... | collective-permute-start | bytes 786440 | tf_op jit(solution)/shard_map/ppermute | solution.py:142
  60.2 6.9 %collective-permute-start.3 = (f32[256,256]{1,0:T(8,128)S(1)}, f32[256,256]{1,0:T(8,128)S(1)}, u32[]{:S(2)}, u32[]{:S(2)}) collective-permute-start(f32[256,256]{1,0:T(8,128)S(1)} %get-tuple-element.18), channel_id=1, source_target_pairs={{0,16},{16,0},{8,24},{24,8},{1,17},{17,1},{9,25},{25,9},{2,18},{18... | collective-permute-start | bytes 786440 | tf_op jit(solution)/shard_map/ppermute | solution.py:142
  64.7 7.6 %collective-permute-start.5 = (f32[256,256]{1,0:T(8,128)S(1)}, f32[256,256]{1,0:T(8,128)S(1)}, u32[]{:S(2)}, u32[]{:S(2)}) collective-permute-start(f32[256,256]{1,0:T(8,128)S(1)} %collective-permute-done.4), channel_id=1, source_target_pairs={{0,16},{16,0},{8,24},{24,8},{1,17},{17,1},{9,25},{25,9},{2,18},{18... | collective-permute-start | bytes 786440 | tf_op jit(solution)/shard_map/ppermute | solution.py:142
  66.8 29.8 %collective-permute-start.8 = (f32[512,256]{1,0:T(8,128)S(1)}, f32[512,256]{1,0:T(8,128)S(1)}, u32[]{:S(2)}, u32[]{:S(2)}) collective-permute-start(f32[512,256]{1,0:T(8,128)S(1)} %slice.78), channel_id=1, source_target_pairs={{0,4},{4,0},{1,5},{5,1},{2,6},{6,2},{3,7},{7,3},{8,12},{12,8},{9,1... | collective-permute-start | bytes 1572872 | tf_op jit(solution)/shard_map/ppermute | solution.py:142
  72.3 40.1 %collective-permute-start.6 = (f32[512,256]{1,0:T(8,128)S(1)}, f32[512,256]{1,0:T(8,128)S(1)}, u32[]{:S(2)}, u32[]{:S(2)}) collective-permute-start(f32[512,256]{1,0:T(8,128)S(1)} %slice.77), channel_id=1, source_target_pairs={{0,16},{16,0},{8,24},{24,8},{1,17},{17,1},{9,25},{25,9},{2,18},{18... | collective-permute-start | bytes 1572872 | tf_op jit(solution)/shard_map/ppermute | solution.py:142
  96.6 12.9 %collective-permute-start.9 = (f32[256,256]{1,0:T(8,128)S(1)}, f32[256,256]{1,0:T(8,128)S(1)}, u32[]{:S(2)}, u32[]{:S(2)}) collective-permute-start(f32[256,256]{1,0:T(8,128)S(1)} %get-tuple-element.24), channel_id=1, source_target_pairs={{0,4},{4,0},{1,5},{5,1},{2,6},{6,2},{3,7},{7,3},{8,12},{12,8},{9,1... | collective-permute-start | bytes 786440 | tf_op jit(solution)/shard_map/ppermute | solution.py:142
  97.6 15.9 %collective-permute-start.11 = (f32[512,256]{1,0:T(8,128)S(1)}, f32[512,256]{1,0:T(8,128)S(1)}, u32[]{:S(2)}, u32[]{:S(2)}) collective-permute-start(f32[512,256]{1,0:T(8,128)S(1)} %collective-permute-done.8), channel_id=1, source_target_pairs={{0,16},{16,0},{8,24},{24,8},{1,17},{17,1},{9,25},{25,9},{2,18},{18... | collective-permute-start | bytes 1572872 | tf_op jit(solution)/shard_map/ppermute | solution.py:142
  109.6 13.8 %collective-permute-start.10 = (f32[512,256]{1,0:T(8,128)S(1)}, f32[512,256]{1,0:T(8,128)S(1)}, u32[]{:S(2)}, u32[]{:S(2)}) collective-permute-start(f32[512,256]{1,0:T(8,128)S(1)} %constant_dynamic-update-slice_fusion), channel_id=1, source_target_pairs={{0,16},{16,0},{8,24},{24,8},{1,17},{17,1},{9,25},{25,9},{2,18},{18... | collective-permute-start | bytes 1572872 | tf_op jit(solution)/shard_map/ppermute | solution.py:142
  110.3 2.2 %slice-start = ((f32[768,256]{1,0:T(8,128)}), f32[512,256]{1,0:T(8,128)S(1)}, s32[]{:S(2)}) async-start(f32[768,256]{1,0:T(8,128)} %copy-done.7), calls=%async_computation | async-start | bytes 1048576 | tf_op jit(solution)/shard_map/slice | solution.py:215
  111.4 14.1 %copy-start.5 = (f32[512,512]{1,0:T(8,128)}, f32[512,512]{1,0:T(8,128)S(1)}, u32[]{:S(2)}) copy-start(f32[512,512]{1,0:T(8,128)S(1)} %fusion.13) | copy-start | bytes 3145732
